TPU v7x, 32 devices: a whole 2x2x4 slice. The times are simulated.
32 devices in a mesh: dp: 2 (over y), expert: 4 (over x, core), tensor: 4 (over z).
Axes of the slice: x: 2, y: 2, z: 4, core: 2. Of those that a mesh axis runs over, the one named last changes fastest.
Arguments:
- hidden_states: bfloat16 [256, 4096], P(('dp', 'expert'), 'tensor'), may hold values from -6 to 6
- chosen_experts: int32 [256, 2], P(('dp', 'expert')), may hold values from 0 to 3, all different within a row; in each aligned block of 32 rows (0 to 31, 32 to 63, ...) at most 16 rows name the same one
- choice_weights: float32 [256, 2], P(('dp', 'expert')), may hold values from 0.2 to 1
- gate_proj: bfloat16 [4, 4096, 8192], P('expert', None, ('dp', 'tensor')), may hold values from -0.09375 to 0.09375
- up_proj: bfloat16 [4, 4096, 8192], P('expert', None, ('dp', 'tensor')), may hold values from -0.09375 to 0.09375
- down_proj: bfloat16 [4, 8192, 4096], P('expert', 'dp', 'tensor'), may hold values from -0.0625 to 0.0625
Outputs:
- moe_output: bfloat16 [256, 4096], P(('dp', 'expert'), 'tensor')
Inputs may be any that keep to these rules, and one draw needn't show every extreme that they name: `chosen_experts`: each row names 2 different experts; among the 32 rows of one device no expert is named more than 16 times, a bound that some block reaches.
All inputs are finite; a program needn't handle non-finite values.
Results may differ from a plain program's by a relative error of at most 0.0058.
Values may be sent and summed in bfloat16 or wider, within the bound.
A program may use at most 64 MiB of HBM per device.

v0:
```python
import jax
import jax.numpy as jnp
from jax import lax
from jax.sharding import PartitionSpec as P

CAP = 16


def slot_tables(chosen_experts, experts, capacity):
    flat_ids = chosen_experts.reshape(-1)
    onehot = (flat_ids[:, None] == jnp.arange(experts, dtype=jnp.int32)[None, :]).astype(jnp.int32)
    before = jnp.cumsum(onehot, axis=0) - onehot
    position = jnp.sum(before * onehot, axis=1)
    return (flat_ids * capacity + position).reshape(chosen_experts.shape)


def body(hidden_states, chosen_experts, choice_weights, gate_proj, up_proj, down_proj):
    experts = lax.axis_size("expert")
    token_count = hidden_states.shape[0]
    feat_width = hidden_states.shape[1]
    slot_count = experts * CAP
    target = slot_tables(chosen_experts, experts, CAP)
    slot_ids = jnp.arange(slot_count, dtype=jnp.int32)
    placing = jnp.zeros((slot_count, token_count), jnp.float32)
    weights_table = jnp.zeros((token_count, slot_count), jnp.float32)
    for column in range(target.shape[1]):
        placing = placing + (slot_ids[:, None] == target[None, :, column]).astype(jnp.float32)
        weights_table = weights_table + jnp.where(
            target[:, column][:, None] == slot_ids[None, :],
            choice_weights[:, column][:, None],
            jnp.float32(0.0),
        )
    packed = jnp.dot(
        placing.astype(jnp.bfloat16), hidden_states, preferred_element_type=jnp.float32
    )
    packed = packed.astype(jnp.bfloat16).reshape(experts, CAP, feat_width)
    arrived = lax.all_to_all(packed, "expert", split_axis=0, concat_axis=0, tiled=True).reshape(
        slot_count, feat_width
    )
    gate_weights = gate_proj[0]
    up_weights = up_proj[0]
    down_weights = down_proj[0]
    features = lax.all_gather(arrived, "tensor", axis=1, tiled=True)
    shards = lax.all_gather(features, "dp", axis=0, tiled=True)
    gate_part = jnp.dot(shards, gate_weights, preferred_element_type=jnp.float32)
    up_part = jnp.dot(shards, up_weights, preferred_element_type=jnp.float32)
    activated = (jax.nn.silu(gate_part) * up_part).astype(jnp.bfloat16)
    unit_rows = lax.all_gather(activated, "tensor", axis=1, tiled=True)
    summed = lax.psum_scatter(
        jnp.dot(unit_rows, down_weights, preferred_element_type=jnp.float32),
        "dp",
        scatter_dimension=0,
        tiled=True,
    )
    outgoing = summed.astype(jnp.bfloat16).reshape(experts, CAP, feat_width)
    returned = lax.all_to_all(outgoing, "expert", split_axis=0, concat_axis=0, tiled=True).reshape(
        slot_count, feat_width
    )
    combined = jnp.dot(
        weights_table,
        returned.astype(jnp.float32),
        precision=lax.Precision.HIGHEST,
        preferred_element_type=jnp.float32,
    )
    return combined.astype(jnp.bfloat16)


def solution(mesh):
    in_specs = (
        P(("dp", "expert"), "tensor"),
        P(("dp", "expert"), None),
        P(("dp", "expert"), None),
        P("expert", None, ("dp", "tensor")),
        P("expert", None, ("dp", "tensor")),
        P("expert", "dp", "tensor"),
    )
    out_specs = P(("dp", "expert"), "tensor")
    return jax.shard_map(body, mesh=mesh, in_specs=in_specs, out_specs=out_specs, check_vma=False)
```

profile of v0, /device:TPU:0, one launch (start us, length us, event | category | flops | bytes accessed | tf_op | source)
XLA Modules:
  0.0 131.8 jit_solution(14651087666373031079)
XLA Ops:
  6.5 0.0 copy-start
  6.5 0.0 all-gather.3.cloned.1.call-start
  6.5 0.8 copy.13
  7.3 0.1 eq.71
  7.4 0.1 fusion.12
  7.5 0.1 reduce_window_sum.11
  7.6 0.2 select_reduce_fusion
  7.8 0.1 reduce_sum.12
  7.9 0.1 copy.14
  8.0 0.7 multiply_add_fusion
  8.7 0.0 copy-done
  8.7 0.2 convolution_convert_fusion
  8.9 8.6 %all_to_all.10 = bf16[4,16,1024]{2,1,0:T(8,128)(2,1)S(1)} all-to-all(bf16[4,16,1024]{2,1,0:T(8,128)(2,1)S(1)} %bitcast.31), channel_id=1, replica_groups=mesh['dp'=2,'expert'=4,'tensor'=4] {'expert'}, dimensions={0} | all-to-all | bytes 262144 | tf_op jit(solution)/shard_map/all_to_all | solution.py:37
  17.5 16.2 %all_gather.9 = bf16[64,4096]{1,0:T(8,128)(2,1)} all-gather(bf16[64,1024]{1,0:T(8,128)(2,1)S(1)} %bitcast.30), channel_id=1, replica_groups=mesh['dp'=2,'expert'=4,'tensor'=4] {'tensor'}, dimensions={1}, use_global_device_ids=true | all-gather | bytes 655360 | tf_op jit(solution)/shard_map/all_gather | solution.py:43
  33.8 0.0 all-gather.3.cloned.1.call-update
  33.8 0.0 all-gather.5.cloned.1.call-start
  33.8 22.4 %all-gather.3.cloned.1.call-done = bf16[128,4096]{1,0:T(8,128)(2,1)} async-done(((bf16[64,4096]{1,0:T(8,128)(2,1)}), bf16[128,4096]{1,0:T(8,128)(2,1)}) %all-gather.3.cloned.1.call-update) | async-done | bytes 1048592 | tf_op jit(solution)/shard_map/all_gather | solution.py:44
  56.2 0.0 copy-start.1
  56.2 5.0 %fusion.4 = f32[128,1024]{1,0:T(8,128)S(1)} fusion(bf16[128,4096]{1,0:T(8,128)(2,1)} %all-gather.3.cloned.1.call-done, bf16[1,4096,1024]{2,1,0:T(8,128)(2,1)} %param.9), kind=kOutput, calls=%fused_computation.4 | convolution fusion | flops 1073741824 | bytes 9961472 | tf_op jit(solution)/shard_map/dot_general | solution.py:45
  61.2 0.0 copy-done.1
  61.2 5.5 %fusion.9 = bf16[128,1024]{1,0:T(8,128)(2,1)} fusion(bf16[128,4096]{1,0:T(8,128)(2,1)S(1)} %copy-done.1, bf16[1,4096,1024]{2,1,0:T(8,128)(2,1)} %param.10, f32[128,1024]{1,0:T(8,128)S(1)} %fusion.4), kind=kOutput, calls=%fused_computation.7 | convolution fusion | flops 1074528256 | bytes 10223616 | tf_op jit(solution)/shard_map/dot_general | solution.py:46
  66.7 0.0 all-gather.5.cloned.1.call-update
  66.8 0.0 copy-start.2
  66.8 0.0 reduce-scatter.2.cloned.1.call-start
  66.8 28.0 %all-gather.5.cloned.1.call-done = bf16[128,4096]{1,0:T(8,128)(2,1)} async-done(((bf16[128,1024]{1,0:T(8,128)(2,1)}), bf16[128,4096]{1,0:T(8,128)(2,1)}) %all-gather.5.cloned.1.call-update) | async-done | bytes 1048592 | tf_op jit(solution)/shard_map/all_gather | solution.py:48
  94.8 5.8 %fusion = f32[128,1024]{1,0:T(8,128)} fusion(bf16[128,4096]{1,0:T(8,128)(2,1)} %all-gather.5.cloned.1.call-done, bf16[1,4096,1024]{2,1,0:T(8,128)(2,1)} %param.11), kind=kOutput, calls=%fused_computation | convolution fusion | flops 1073741824 | bytes 9961472 | tf_op jit(solution)/shard_map/dot_general | solution.py:50
  100.6 0.0 reduce-scatter.2.cloned.1.call-update
  100.7 14.2 %reduce-scatter.2.cloned.1.call-done = f32[64,1024]{1,0:T(8,128)} async-done(((f32[128,1024]{1,0:T(8,128)}), f32[64,1024]{1,0:T(8,128)}) %reduce-scatter.2.cloned.1.call-update) | async-done | bytes 262160 | tf_op jit(solution)/shard_map/reduce_scatter | solution.py:49
  114.9 1.6 %convert_element_type.31 = bf16[64,1024]{1,0:T(8,128)(2,1)} convert(f32[64,1024]{1,0:T(8,128)} %reduce-scatter.2.cloned.1.call-done) | non-fusion elementwise | flops 65536 | bytes 393216 | tf_op jit(solution)/shard_map/convert_element_type | solution.py:55
  116.5 3.3 %all-to-all-start.1 = ((bf16[4,16,1024]{2,1,0:T(8,128)(2,1)}), bf16[4,16,1024]{2,1,0:T(8,128)(2,1)S(1)}, u32[]{:S(2)}, u32[]{:S(2)}) async-start(bf16[4,16,1024]{2,1,0:T(8,128)(2,1)} %bitcast.9), calls=%async_computation.2 | async-start | bytes 262144 | tf_op jit(solution)/shard_map/all_to_all | solution.py:56
  119.8 0.0 copy-done.2
  119.8 4.6 %all-to-all-done.1 = bf16[4,16,1024]{2,1,0:T(8,128)(2,1)S(1)} async-done(((bf16[4,16,1024]{2,1,0:T(8,128)(2,1)}), bf16[4,16,1024]{2,1,0:T(8,128)(2,1)S(1)}, u32[]{:S(2)}, u32[]{:S(2)}) %all-to-all-start.1) | async-done | bytes 131104 | tf_op jit(solution)/shard_map/all_to_all | solution.py:56
  124.4 0.9 convolution_convert_fusion.1
  (2 shorter events, 0.0 us)
Async XLA Ops:
  6.5 2.2 %copy-start = (bf16[32,1024]{1,0:T(8,128)(2,1)S(1)}, bf16[32,1024]{1,0:T(8,128)(2,1)}, u32[]{:S(2)}) copy-start(bf16[32,1024]{1,0:T(8,128)(2,1)} %param.6) | copy-start | bytes 196612
  6.5 49.7 %all-gather.3.cloned.1.call-start = ((), (), s32[]{:S(2)}) async-start(), calls=%async_computation.3 | async-start | bytes 1572864 | tf_op jit(solution)/shard_map/all_gather | solution.py:44
  33.8 61.1 %all-gather.5.cloned.1.call-start = ((), (), s32[]{:S(2)}) async-start(), calls=%async_computation.4 | async-start | bytes 1310720 | tf_op jit(solution)/shard_map/all_gather | solution.py:48
  56.2 5.0 %copy-start.1 = (bf16[128,4096]{1,0:T(8,128)(2,1)S(1)}, bf16[128,4096]{1,0:T(8,128)(2,1)}, u32[]{:S(2)}) copy-start(bf16[128,4096]{1,0:T(8,128)(2,1)} %all-gather.3.cloned.1.call-done) | copy-start | bytes 3145732
  66.8 53.1 %copy-start.2 = (f32[32,2]{0,1:T(2,128)S(1)}, f32[32,2]{0,1:T(2,128)}, u32[]{:S(2)}) copy-start(f32[32,2]{0,1:T(2,128)} %param.8) | copy-start | bytes 772
  66.8 48.1 %reduce-scatter.2.cloned.1.call-start = ((), (), s32[]{:S(2)}) async-start(), calls=%async_computation.5 | async-start | bytes 786432 | tf_op jit(solution)/shard_map/reduce_scatter | solution.py:49
  116.5 7.9 %all-to-all-start.1 = ((bf16[4,16,1024]{2,1,0:T(8,128)(2,1)}), bf16[4,16,1024]{2,1,0:T(8,128)(2,1)S(1)}, u32[]{:S(2)}, u32[]{:S(2)}) async-start(bf16[4,16,1024]{2,1,0:T(8,128)(2,1)} %bitcast.9), calls=%async_computation.2 | async-start | bytes 262144 | tf_op jit(solution)/shard_map/all_to_all | solution.py:56
Sparse Core Ops, SparseCore 0:
  33.9 22.2 all-gather.2
  66.9 27.9 all-gather.4
  100.8 14.0 reduce-scatter.1
where the time goes:
time: 132 us
  waiting for transfers between devices  69.2 us (52%)
  blocking collectives  24.9 us (19%)
  matrix products  17.4 us (13%)
  between operations  13.2 us (10%)
  starting transfers between devices  3.41 us (3%)
  other arithmetic  2.66 us (2%)
    all_gather x1, waiting for transfers between devices, body(): unit_rows = lax.all_gather(activated, 'tensor', axis=1, tiled=True)  28 us
    all_gather x1, waiting for transfers between devices, body(): shards = lax.all_gather(features, 'dp', axis=0, tiled=True)  22.4 us
    all_gather x1, blocking collectives, body(): features = lax.all_gather(arrived, 'tensor', axis=1, tiled=True)  16.2 us
    reduce_scatter x1, waiting for transfers between devices, body(): lax.psum_scatter(jnp.dot(unit_rows, down_weights, preferred_element_type=...  14.2 us
    all_to_all x1, blocking collectives, body(): lax.all_to_all(packed, 'expert', split_axis=0, concat_axis=0, tiled=True)  8.64 us
    dot_general x1, matrix products, body(): jnp.dot(unit_rows, down_weights, preferred_element_type=jnp.float32)  5.79 us
    dot_general x1, matrix products, body(): up_part = jnp.dot(shards, up_weights, preferred_element_type=jnp.float32)  5.48 us
    dot_general x1, matrix products, body(): jnp.dot(shards, gate_weights, preferred_element_type=jnp.float32)  5.03 us
  transfers between devices with their start and end apart: 4, of which 4 were waited for; matrix products, arithmetic and copies ran while one was open for 0% of the time, Pallas kernels for 0%

commit v1 on v0

--- a/solution.py
+++ b/solution.py
@@ -41,7 +41,15 @@
     up_weights = up_proj[0]
     down_weights = down_proj[0]
     features = lax.all_gather(arrived, "tensor", axis=1, tiled=True)
-    shards = lax.all_gather(features, "dp", axis=0, tiled=True)
+    ways, here = (lax.axis_size("dp"), lax.axis_index("dp"))
+    grown, reach = (features, 1)
+    while reach < ways:
+        theirs = lax.ppermute(grown, "dp", [(d, d ^ reach) for d in range(ways)])
+        mine_first = jnp.concatenate([grown, theirs], axis=0)
+        theirs_first = jnp.concatenate([theirs, grown], axis=0)
+        grown = jnp.where(here & reach == 0, mine_first, theirs_first)
+        reach = 2 * reach
+    shards = grown
     gate_part = jnp.dot(shards, gate_weights, preferred_element_type=jnp.float32)
     up_part = jnp.dot(shards, up_weights, preferred_element_type=jnp.float32)
     activated = (jax.nn.silu(gate_part) * up_part).astype(jnp.bfloat16)

time: 132 us -> 120 us (0.909)
  waiting for transfers between devices: 69.2 us -> 56.4 us
  starting transfers between devices: 3.41 us -> 4.89 us
    all_gather x1 -> x0, waiting for transfers between devices: 22.4 us -> none  [body(): shards = lax.all_gather(features, 'dp', axis=0, tiled=True)]
    ppermute x0 -> x1, waiting for transfers between devices: none -> 9.77 us  [body(): theirs = lax.ppermute(grown, 'dp', [(d, d ^ reach) for d in range(ways)])]
    ppermute x0 -> x1, starting transfers between devices: none -> 1.52 us  [body(): theirs = lax.ppermute(grown, 'dp', [(d, d ^ reach) for d in range(ways)])]
where the time goes in v1:
time: 120 us
  waiting for transfers between devices  56.4 us (47%)
  blocking collectives  24.3 us (20%)
  matrix products  17 us (14%)
  between operations  13.5 us (11%)
  starting transfers between devices  4.89 us (4%)
  other arithmetic  2.66 us (2%)
    all_gather x1, waiting for transfers between devices, body(): unit_rows = lax.all_gather(activated, 'tensor', axis=1, tiled=True)  27.8 us
    all_gather x1, blocking collectives, body(): features = lax.all_gather(arrived, 'tensor', axis=1, tiled=True)  15.6 us
    reduce_scatter x1, waiting for transfers between devices, body(): lax.psum_scatter(jnp.dot(unit_rows, down_weights, preferred_element_type=...  14.2 us
    ppermute x1, waiting for transfers between devices, body(): theirs = lax.ppermute(grown, 'dp', [(d, d ^ reach) for d in range(ways)])  9.77 us
    all_to_all x1, blocking collectives, body(): lax.all_to_all(packed, 'expert', split_axis=0, concat_axis=0, tiled=True)  8.64 us
    dot_general x1, matrix products, body(): jnp.dot(unit_rows, down_weights, preferred_element_type=jnp.float32)  5.79 us
    dot_general x1, matrix products, body(): up_part = jnp.dot(shards, up_weights, preferred_element_type=jnp.float32)  5.45 us
    dot_general x1, matrix products, body(): jnp.dot(shards, gate_weights, preferred_element_type=jnp.float32)  4.68 us
  transfers between devices with their start and end apart: 4, of which 4 were waited for; matrix products, arithmetic and copies ran while one was open for 0% of the time, Pallas kernels for 0%

profile of v1, /device:TPU:0, one launch (start us, length us, event | category | flops | bytes accessed | tf_op | source)
XLA Modules:
  0.0 119.8 jit_solution(16973471661101983111)
XLA Ops:
  6.5 0.0 copy-start
  6.5 0.0 all-gather.2.cloned.1.call-start
  6.5 0.8 copy.13
  7.3 0.1 eq.74
  7.4 0.1 fusion.8
  7.5 0.1 reduce_window_sum.11
  7.6 0.2 select_reduce_fusion
  7.8 0.1 reduce_sum.12
  7.9 0.1 copy.14
  8.0 0.7 multiply_add_fusion
  8.7 0.0 copy-done
  8.7 0.2 convolution_convert_fusion
  8.9 8.6 %all_to_all.10 = bf16[4,16,1024]{2,1,0:T(8,128)(2,1)S(1)} all-to-all(bf16[4,16,1024]{2,1,0:T(8,128)(2,1)S(1)} %bitcast.27), channel_id=1, replica_groups=mesh['dp'=2,'expert'=4,'tensor'=4] {'expert'}, dimensions={0} | all-to-all | bytes 262144 | tf_op jit(solution)/shard_map/all_to_all | solution.py:37
  17.5 15.6 %all_gather.6 = bf16[64,4096]{1,0:T(8,128)(2,1)S(1)} all-gather(bf16[64,1024]{1,0:T(8,128)(2,1)S(1)} %bitcast.26), channel_id=1, replica_groups=mesh['dp'=2,'expert'=4,'tensor'=4] {'tensor'}, dimensions={1}, use_global_device_ids=true | all-gather | bytes 655360 | tf_op jit(solution)/shard_map/all_gather | solution.py:43
  33.1 1.5 %collective-permute-start = (bf16[64,4096]{1,0:T(8,128)(2,1)S(1)}, bf16[64,4096]{1,0:T(8,128)(2,1)S(1)}, u32[]{:S(2)}, u32[]{:S(2)}) collective-permute-start(bf16[64,4096]{1,0:T(8,128)(2,1)S(1)} %all_gather.6), channel_id=1, source_target_pairs={{0,16},{16,0},{1,17},{17,1},{2,18},{18,2},{3,19},{19,3},{4,20},{20... | collective-permute-start | bytes 1572872 | tf_op jit(solution)/shard_map/ppermute | solution.py:47
  34.7 9.8 %collective-permute-done = bf16[64,4096]{1,0:T(8,128)(2,1)S(1)} collective-permute-done((bf16[64,4096]{1,0:T(8,128)(2,1)S(1)}, bf16[64,4096]{1,0:T(8,128)(2,1)S(1)}, u32[]{:S(2)}, u32[]{:S(2)}) %collective-permute-start) | collective-permute-done | bytes 524320 | tf_op jit(solution)/shard_map/ppermute | solution.py:47
  44.4 4.7 %fusion.4 = f32[128,1024]{1,0:T(8,128)S(1)} fusion(bf16[1,4096,1024]{2,1,0:T(8,128)(2,1)} %param.9, bf16[64,4096]{1,0:T(8,128)(2,1)S(1)} %collective-permute-done, bf16[64,4096]{1,0:T(8,128)(2,1)S(1)} %all_gather.6, pred[]{:T(512)S(6)} %eq.86), kind=kOutput, calls=%fused_computation.4 | convolution fusion | flops 1078460416 | bytes 9961473 | tf_op jit(solution)/shard_map/dot_general | solution.py:53
  49.1 5.5 %multiply_convert_fusion = bf16[128,1024]{1,0:T(8,128)(2,1)} fusion(f32[128,1024]{1,0:T(8,128)S(1)} %fusion.4, bf16[1,4096,1024]{2,1,0:T(8,128)(2,1)} %param.10, bf16[64,4096]{1,0:T(8,128)(2,1)S(1)} %collective-permute-done, bf16[64,4096]{1,0:T(8,128)(2,1)S(1)} %all_gather.6, pred[]{:T(512)S(6)} %eq.86), kind=kOutput, calls=%fused_computation.9 | convolution fusion | flops 1079246848 | bytes 10223617 | tf_op jit(solution)/shard_map/dot_general | solution.py:54
  54.6 0.0 all-gather.2.cloned.1.call-update
  54.6 0.0 copy-start.1
  54.6 0.0 reduce-scatter.2.cloned.1.call-start
  54.7 27.8 %all-gather.2.cloned.1.call-done = bf16[128,4096]{1,0:T(8,128)(2,1)} async-done(((bf16[128,1024]{1,0:T(8,128)(2,1)}), bf16[128,4096]{1,0:T(8,128)(2,1)}) %all-gather.2.cloned.1.call-update) | async-done | bytes 1048592 | tf_op jit(solution)/shard_map/all_gather | solution.py:56
  82.5 5.8 %fusion = f32[128,1024]{1,0:T(8,128)} fusion(bf16[128,4096]{1,0:T(8,128)(2,1)} %all-gather.2.cloned.1.call-done, bf16[1,4096,1024]{2,1,0:T(8,128)(2,1)} %param.11), kind=kOutput, calls=%fused_computation | convolution fusion | flops 1073741824 | bytes 9961472 | tf_op jit(solution)/shard_map/dot_general | solution.py:58
  88.3 0.0 reduce-scatter.2.cloned.1.call-update
  88.3 14.2 %reduce-scatter.2.cloned.1.call-done = f32[64,1024]{1,0:T(8,128)} async-done(((f32[128,1024]{1,0:T(8,128)}), f32[64,1024]{1,0:T(8,128)}) %reduce-scatter.2.cloned.1.call-update) | async-done | bytes 262160 | tf_op jit(solution)/shard_map/reduce_scatter | solution.py:57
  102.5 1.6 %convert_element_type.31 = bf16[64,1024]{1,0:T(8,128)(2,1)} convert(f32[64,1024]{1,0:T(8,128)} %reduce-scatter.2.cloned.1.call-done) | non-fusion elementwise | flops 65536 | bytes 393216 | tf_op jit(solution)/shard_map/convert_element_type | solution.py:63
  104.1 3.3 %all-to-all-start.1 = ((bf16[4,16,1024]{2,1,0:T(8,128)(2,1)}), bf16[4,16,1024]{2,1,0:T(8,128)(2,1)S(1)}, u32[]{:S(2)}, u32[]{:S(2)}) async-start(bf16[4,16,1024]{2,1,0:T(8,128)(2,1)} %bitcast.9), calls=%async_computation.2 | async-start | bytes 262144 | tf_op jit(solution)/shard_map/all_to_all | solution.py:64
  107.4 0.0 copy-done.1
  107.5 4.6 %all-to-all-done.1 = bf16[4,16,1024]{2,1,0:T(8,128)(2,1)S(1)} async-done(((bf16[4,16,1024]{2,1,0:T(8,128)(2,1)}), bf16[4,16,1024]{2,1,0:T(8,128)(2,1)S(1)}, u32[]{:S(2)}, u32[]{:S(2)}) %all-to-all-start.1) | async-done | bytes 131104 | tf_op jit(solution)/shard_map/all_to_all | solution.py:64
  112.0 0.9 convolution_convert_fusion.1
  (2 shorter events, 0.0 us)
Async XLA Ops:
  6.5 2.2 %copy-start = (bf16[32,1024]{1,0:T(8,128)(2,1)S(1)}, bf16[32,1024]{1,0:T(8,128)(2,1)}, u32[]{:S(2)}) copy-start(bf16[32,1024]{1,0:T(8,128)(2,1)} %param.6) | copy-start | bytes 196612
  6.5 75.9 %all-gather.2.cloned.1.call-start = ((), (), s32[]{:S(2)}) async-start(), calls=%async_computation.3 | async-start | bytes 1310720 | tf_op jit(solution)/shard_map/all_gather | solution.py:56
  33.1 11.3 %collective-permute-start = (bf16[64,4096]{1,0:T(8,128)(2,1)S(1)}, bf16[64,4096]{1,0:T(8,128)(2,1)S(1)}, u32[]{:S(2)}, u32[]{:S(2)}) collective-permute-start(bf16[64,4096]{1,0:T(8,128)(2,1)S(1)} %all_gather.6), channel_id=1, source_target_pairs={{0,16},{16,0},{1,17},{17,1},{2,18},{18,2},{3,19},{19,3},{4,20},{20... | collective-permute-start | bytes 1572872 | tf_op jit(solution)/shard_map/ppermute | solution.py:47
  54.6 52.8 %copy-start.1 = (f32[32,2]{0,1:T(2,128)S(1)}, f32[32,2]{0,1:T(2,128)}, u32[]{:S(2)}) copy-start(f32[32,2]{0,1:T(2,128)} %param.8) | copy-start | bytes 772
  54.6 47.9 %reduce-scatter.2.cloned.1.call-start = ((), (), s32[]{:S(2)}) async-start(), calls=%async_computation.4 | async-start | bytes 786432 | tf_op jit(solution)/shard_map/reduce_scatter | solution.py:57
  104.1 7.9 %all-to-all-start.1 = ((bf16[4,16,1024]{2,1,0:T(8,128)(2,1)}), bf16[4,16,1024]{2,1,0:T(8,128)(2,1)S(1)}, u32[]{:S(2)}, u32[]{:S(2)}) async-start(bf16[4,16,1024]{2,1,0:T(8,128)(2,1)} %bitcast.9), calls=%async_computation.2 | async-start | bytes 262144 | tf_op jit(solution)/shard_map/all_to_all | solution.py:64
Sparse Core Ops, SparseCore 0:
  54.7 27.7 all-gather.1
  88.4 14.0 reduce-scatter.1
